TPU v7x, 32 devices: a whole 2x2x4 slice. The times are simulated.
32 devices in a mesh: seg: 4 (over y, x), gx: 2 (over core), gy: 4 (over z).
Axes of the slice: x: 2, y: 2, z: 4, core: 2. Of those that a mesh axis runs over, the one named last changes fastest.
Arguments:
- gas_state: float32 [7, 384, 32, 512], P(None, 'seg', 'gx', 'gy'), may hold values from 0 to 1
- solids_temp: float32 [384, 32, 512], P('seg', 'gx', 'gy'), may hold values from 0.2 to 1.2
- exchange_rate: float32 [32, 512], P('gx', 'gy'), may hold values from 0.1 to 0.5
- column_flags: int32 [32, 512], P('gx', 'gy'), may hold values from 0 to 3
- block_inverse: float32 [384, 96], P('seg'), may hold values from -1 to 2, as said below
- line_coupling: float32 [4, 2], P('seg'), may hold values from 0.05 to 0.25
Outputs:
- gas_next: float32 [7, 384, 32, 512], P(None, 'seg', 'gx', 'gy')
- solids_next: float32 [384, 32, 512], P('seg', 'gx', 'gy')
Inputs may be any that keep to these rules, and one draw needn't show every extreme that they name: `block_inverse`: each block of 96 rows holds the inverse of that segment's diagonal block.
All inputs are finite; a program needn't handle non-finite values.
Results may differ from a plain program's by a relative error of at most 0.000061.
Values sent between devices are 32-bit elements; how exact they have to be, the bound alone decides.
A program may use at most 192 MiB of HBM per device.

v0:
```python
import jax
import jax.numpy as jnp
from jax import lax
from jax.sharding import PartitionSpec as P

diffusion = (0.1, 0.08, 0.12, 0.09, 0.11, 0.07)
stoich = (-1.0, -0.5, 1.0, 0.5, 0.25, 0.75)
rate_const = 0.3
upwind = 0.25
cond_base = 0.04
cond_slope = 0.3
heat_release = 0.5
lateral = 0.1
loss_table = (0.0, 0.3, 0.0, 0.1)
feed_table = (0.0, 0.0, 0.4, 0.0)
highest = lax.Precision.HIGHEST


def with_halo(block, sides, width):
    for axis, dim in sides:
        count = lax.axis_size(axis)
        forward = [(i, i + 1) for i in range(count - 1)]
        backward = [(target, source) for source, target in forward]
        low = lax.ppermute(
            lax.slice_in_dim(block, block.shape[dim] - width, None, axis=dim), axis, forward
        )
        high = lax.ppermute(lax.slice_in_dim(block, 0, width, axis=dim), axis, backward)
        block = jnp.concatenate([low, block, high], axis=dim)
    return block


def advance_species(padded, spread, gains, reaction):
    center = padded[:, 1:-1, 1:-1, 1:-1]
    beside = padded[:, 2:, 1:-1, 1:-1] + padded[:, :-2, 1:-1, 1:-1]
    beside = beside + padded[:, 1:-1, 2:, 1:-1] + padded[:, 1:-1, :-2, 1:-1]
    beside = beside + padded[:, 1:-1, 1:-1, 2:] + padded[:, 1:-1, 1:-1, :-2]
    below = padded[:, :-2, 1:-1, 1:-1]
    return (
        center
        + spread * (beside - 6.0 * center)
        - upwind * (center - below)
        + gains * reaction[None]
    )


def lookup(flags, table):
    result = jnp.zeros(flags.shape, jnp.float32)
    for value, entry in enumerate(table):
        result = result + jnp.where(flags == value, entry, 0.0)
    return result


def advance_enthalpy(heat_pad, mix_pad, reaction, flags):
    cond = cond_base + cond_slope * mix_pad
    heat_mid = heat_pad[1:-1, 1:-1, 1:-1]
    cond_mid = cond[1:-1, 1:-1, 1:-1]
    flux = jnp.zeros(heat_mid.shape, heat_mid.dtype)
    views = (
        (slice(2, None), slice(1, -1), slice(1, -1)),
        (slice(None, -2), slice(1, -1), slice(1, -1)),
        (slice(1, -1), slice(2, None), slice(1, -1)),
        (slice(1, -1), slice(None, -2), slice(1, -1)),
        (slice(1, -1), slice(1, -1), slice(2, None)),
        (slice(1, -1), slice(1, -1), slice(None, -2)),
    )
    for view in views:
        flux = flux + 0.5 * (cond_mid + cond[view]) * (heat_pad[view] - heat_mid)
    loss = lookup(flags, loss_table)[None]
    feed = lookup(flags, feed_table)[None]
    return heat_mid + flux + heat_release * reaction - loss * heat_mid + feed


def solid_source(temp_pad, temp, heat_new, exchange):
    beside = (
        temp_pad[:, 2:, 1:-1]
        + temp_pad[:, :-2, 1:-1]
        + temp_pad[:, 1:-1, 2:]
        + temp_pad[:, 1:-1, :-2]
    )
    return temp + lateral * (beside - 4.0 * temp) + exchange[None] * (heat_new - temp)


def reduced_inverse(scalars):
    count = scalars.shape[0]
    size = 2 * count
    index = jnp.arange(size)
    segment = index // 2
    odd = index % 2
    rows = scalars[segment]
    first = jnp.where(odd == 0, rows[:, 0], rows[:, 1]) * rows[:, 4]
    last = jnp.where(odd == 0, rows[:, 2], rows[:, 3]) * rows[:, 5]
    cols = index[None, :]
    matrix = jnp.eye(size, dtype=scalars.dtype)
    matrix = matrix - jnp.where(cols == (2 * segment - 1)[:, None], first[:, None], 0.0)
    matrix = matrix - jnp.where(cols == (2 * segment + 2)[:, None], last[:, None], 0.0)
    inverse = jnp.eye(size, dtype=scalars.dtype)
    for step in range(size):
        pivot_row = matrix[step] / matrix[step, step]
        pivot_inv = inverse[step] / matrix[step, step]
        is_pivot = index == step
        matrix = jnp.where(is_pivot[:, None], pivot_row[None], matrix)
        inverse = jnp.where(is_pivot[:, None], pivot_inv[None], inverse)
        factor = jnp.where(is_pivot, 0.0, matrix[:, step])
        matrix = matrix - factor[:, None] * pivot_row[None]
        inverse = inverse - factor[:, None] * pivot_inv[None]
    return inverse


def body(gas_state, solids_temp, exchange_rate, column_flags, block_inverse, line_coupling):
    species_count = gas_state.shape[0] - 1
    depth, width_x, width_y = solids_temp.shape
    spread = jnp.array(diffusion, jnp.float32)[:, None, None, None]
    gains = jnp.array(stoich, jnp.float32)[:, None, None, None]
    reaction = rate_const * gas_state[0] * gas_state[1]
    temp_pad = with_halo(solids_temp, (("gx", 1), ("gy", 2)), 1)
    padded = with_halo(gas_state, (("seg", 1), ("gx", 2), ("gy", 3)), 1)
    species_new = advance_species(padded[:species_count], spread, gains, reaction)
    mix = 0.5 * jnp.sum(species_new, axis=0)
    mix_pad = with_halo(mix, (("seg", 0), ("gx", 1), ("gy", 2)), 1)
    heat_pad = padded[species_count]
    heat_new = advance_enthalpy(heat_pad, mix_pad, reaction, column_flags)
    gas_next = jnp.concatenate([species_new, heat_new[None]], axis=0)
    source = solid_source(temp_pad, solids_temp, heat_new, exchange_rate)
    local = jnp.dot(block_inverse, source.reshape(depth, width_x * width_y), precision=highest)
    ends = jnp.stack([local[0], local[depth - 1]])
    scalars = jnp.stack(
        [
            block_inverse[0, 0],
            block_inverse[depth - 1, 0],
            block_inverse[0, depth - 1],
            block_inverse[depth - 1, depth - 1],
            line_coupling[0, 0],
            line_coupling[0, 1],
        ]
    )[None]
    segment_id = lax.axis_index("seg")
    all_ends, all_scalars = (
        lax.all_gather(ends, "seg", axis=0, tiled=True),
        lax.all_gather(scalars, "seg", axis=0, tiled=True),
    )
    inverse = reduced_inverse(all_scalars)
    index = jnp.arange(inverse.shape[0])
    select = jnp.stack([index == 2 * segment_id - 1, index == 2 * segment_id + 2]).astype(
        jnp.float32
    )
    picked = jnp.dot(select, inverse, precision=highest)
    near = jnp.dot(picked, all_ends, precision=highest)
    solved = local + line_coupling[0, 0] * near[0][None, :] * block_inverse[:, 0:1]
    solved = solved + line_coupling[0, 1] * near[1][None, :] * block_inverse[:, depth - 1 : depth]
    return (gas_next, solved.reshape(depth, width_x, width_y))


def solution(mesh):
    in_specs = (
        P(None, "seg", "gx", "gy"),
        P("seg", "gx", "gy"),
        P("gx", "gy"),
        P("gx", "gy"),
        P("seg", None),
        P("seg", None),
    )
    out_specs = (P(None, "seg", "gx", "gy"), P("seg", "gx", "gy"))
    return jax.shard_map(body, mesh=mesh, in_specs=in_specs, out_specs=out_specs, check_vma=False)
```

profile of v0, /device:TPU:0, one launch (start us, length us, event | category | flops | bytes accessed | tf_op | source)
XLA Modules:
  0.0 203.1 jit_solution(5789935153862587755)
XLA Ops:
  2.8 6.1 %collective-permute-start.1 = (f32[7,1,16,128]{3,2,1,0:T(8,128)S(1)}, f32[7,1,16,128]{3,2,1,0:T(8,128)}, u32[]{:S(2)}, u32[]{:S(2)}) collective-permute-start(f32[7,1,16,128]{3,2,1,0:T(8,128)S(1)} %get-tuple-element.18), channel_id=1, source_target_pairs={{0,8},{8,16},{16,24},{1,9},{9,17},{17,25},{2,10},{10,18},{18,26},{... | collective-permute-start | bytes 172040 | tf_op jit(solution)/shard_map/ppermute | solution.py:24
  8.9 1.5 copy.47
  12.3 3.0 %collective-permute-start.13 = (f32[96,1,128]{0,2,1:T(8,128)S(1)}, f32[96,1,128]{0,2,1:T(8,128)S(1)}, u32[]{:S(2)}, u32[]{:S(2)}) collective-permute-start(f32[96,1,128]{0,2,1:T(8,128)S(1)} %get-tuple-element.28), channel_id=1, source_target_pairs={{0,4},{1,5},{2,6},{3,7},{8,12},{9,13},{10,14},{11,15},{16,20},{17,... | collective-permute-start | bytes 147464 | tf_op jit(solution)/shard_map/ppermute | solution.py:24
  16.3 1.4 fusion.68
  17.8 1.4 fusion.69
  21.0 4.0 %stack.12 = f32[6]{0:T(128)S(1)} concatenate(f32[1]{0:T(128)} %bitcast.7, f32[1]{0:T(128)} %bitcast.8, f32[1]{0:T(128)} %bitcast.9, f32[1]{0:T(128)} %bitcast.10, f32[1]{0:T(128)} %bitcast.11, f32[1]{0:T(128)} %bitcast.12), dimensions={0} | concatenate | bytes 48 | tf_op jit(solution)/shard_map/stack | solution.py:126
  25.2 7.9 %copy.27 = f32[7,96,16,128]{1,3,2,0:T(8,128)} copy(f32[7,96,16,128]{3,2,1,0:T(8,128)} %param.8) | data formatting | bytes 11010048 | tf_op args[0]
  33.1 9.7 %all-reduce = f32[24]{0:T(128)S(1)} all-reduce(f32[24]{0:T(128)S(1)} %dynamic-update-slice), channel_id=2, replica_groups=mesh['seg'=4,'gx'=2,'gy'=4] {'seg'}, use_global_device_ids=true, to_apply=%add | all-reduce | flops 24 | bytes 192
  61.6 4.5 %copy.29 = f32[7,1,16,128]{1,3,2,0:T(8,128)} copy(f32[7,1,16,128]{3,2,1,0:T(8,128)S(1)} %collective-permute-done) | data formatting | bytes 114688 | tf_op jit(solution)/shard_map/ppermute | solution.py:27
  66.1 5.2 %copy.30 = f32[7,1,16,128]{1,3,2,0:T(8,128)} copy(f32[7,1,16,128]{3,2,1,0:T(8,128)} %collective-permute-done.1) | data formatting | bytes 114688 | tf_op jit(solution)/shard_map/ppermute | solution.py:24
  71.2 2.4 %pad_maximum_fusion.33 = (f32[7,98,1,128]{1,3,2,0:T(8,128)S(1)}, f32[7,98,1,128]{1,3,2,0:T(8,128)S(1)}) fusion(f32[7,1,16,128]{1,3,2,0:T(8,128)} %copy.29, f32[7,96,16,128]{1,3,2,0:T(8,128)} %copy.27, f32[7,1,16,128]{1,3,2,0:T(8,128)} %copy.30), kind=kLoop, calls=%fused_computation.92 | loop fusion | flops 351232 | bytes 6322176 | tf_op jit(solution)/shard_map/concatenate | solution.py:28
  73.7 1.6 collective-permute-start.2
  75.2 3.1 %collective-permute-start.3 = (f32[7,98,1,128]{1,3,2,0:T(8,128)S(1)}, f32[7,98,1,128]{1,3,2,0:T(8,128)S(1)}, u32[]{:S(2)}, u32[]{:S(2)}) collective-permute-start(f32[7,98,1,128]{1,3,2,0:T(8,128)S(1)} %get-tuple-element.16), channel_id=1, source_target_pairs={{0,4},{1,5},{2,6},{3,7},{8,12},{9,13},{10,14},{11,15},{16,20},{17,... | collective-permute-start | bytes 1053704 | tf_op jit(solution)/shard_map/ppermute | solution.py:24
  79.7 1.9 pad_maximum_fusion.39
  81.6 1.3 collective-permute-start.4
  82.9 4.7 %collective-permute-start.5 = (f32[7,98,18,1]{1,3,2,0:T(1,128)S(1)}, f32[7,98,18,1]{1,3,2,0:T(1,128)S(1)}, u32[]{:S(2)}, u32[]{:S(2)}) collective-permute-start(f32[7,98,18,1]{1,3,2,0:T(1,128)S(1)} %get-tuple-element.14), channel_id=1, source_target_pairs={{0,1},{1,2},{2,3},{4,5},{5,6},{6,7},{8,9},{9,10},{10,11},{12,13},{... | collective-permute-start | bytes 148184 | tf_op jit(solution)/shard_map/ppermute | solution.py:24
  89.4 48.4 %fusion.62 = (f32[96,16,128]{0,2,1:T(8,128)S(1)}, f32[6,96,16,128]{1,3,2,0:T(8,128)}) fusion(f32[96,16,128]{0,2,1:T(8,128)} %fusion.40, f32[6]{0:T(128)S(1)} %copy-done.13, f32[7,98,1,128]{1,3,2,0:T(8,128)} %copy-done.3, f32[7,1,16,128]{1,3,2,0:T(8,128)} %copy.29, f32[7,96,16,128]{1,3,2,0:T(8,128)} %copy.27, f32[7,1,16,128]{1,3,2,0:T(8,128)} %copy.30, ...), kind=kLoop, calls=%fused_computation.222 | loop fusion | flops 38731776 | bytes 35881488 | tf_op jit(solution)/shard_map/reduce_sum | solution.py:118
  138.6 1.7 collective-permute-start.6
  140.6 1.3 collective-permute-start.7
  143.0 4.3 %collective-permute-done.7 = f32[1,16,128]{2,1,0:T(8,128)S(1)} collective-permute-done((f32[1,16,128]{2,1,0:T(8,128)S(1)}, f32[1,16,128]{2,1,0:T(8,128)S(1)}, u32[]{:S(2)}, u32[]{:S(2)}) %collective-permute-start.7) | collective-permute-done | bytes 8224 | tf_op jit(solution)/shard_map/ppermute | solution.py:27
  147.9 1.4 collective-permute-start.8
  149.3 1.3 collective-permute-start.9
  151.5 1.3 collective-permute-start.14
  152.8 4.9 %collective-permute-start.15 = (f32[96,18,1]{0,2,1:T(1,128)S(1)}, f32[96,18,1]{0,2,1:T(1,128)S(1)}, u32[]{:S(2)}, u32[]{:S(2)}) collective-permute-start(f32[96,18,1]{0,2,1:T(1,128)S(1)} %get-tuple-element.25), channel_id=1, source_target_pairs={{0,1},{1,2},{2,3},{4,5},{5,6},{6,7},{8,9},{9,10},{10,11},{12,13},{... | collective-permute-start | bytes 20744 | tf_op jit(solution)/shard_map/ppermute | solution.py:24
  157.9 3.9 %collective-permute-start.10 = (f32[98,18,1]{0,2,1:T(1,128)S(1)}, f32[98,18,1]{0,2,1:T(1,128)S(1)}, u32[]{:S(2)}, u32[]{:S(2)}) collective-permute-start(f32[98,18,1]{0,2,1:T(1,128)S(1)} %get-tuple-element.20), channel_id=1, source_target_pairs={{0,1},{1,2},{2,3},{4,5},{5,6},{6,7},{8,9},{9,10},{10,11},{12,13},{... | collective-permute-start | bytes 21176 | tf_op jit(solution)/shard_map/ppermute | solution.py:24
  161.8 1.6 collective-permute-start.11
  163.5 2.5 %fusion.10 = f32[98,18,130]{0,2,1:T(8,128)S(1)} fusion(f32[7,98,18,1]{1,3,2,0:T(1,128)S(1)} %collective-permute-done.4, f32[7,98,18,1]{1,3,2,0:T(1,128)S(1)} %collective-permute-done.5, f32[7,98,1,128]{1,3,2,0:T(8,128)S(1)} %copy-done.4, f32[7,98,1,128]{1,3,2,0:T(8,128)S(1)} %copy-done.6, f32[7,1,16,128]{1,3,2,0:T(8,128)} %copy.29, ...), kind=kLoop, calls=%fused_computation.32 | loop fusion | flops 1375920 | bytes 7338240 | tf_op jit(solution)/shard_map/squeeze | solution.py:120
  166.0 1.5 collective-permute-done.11
  168.2 6.2 %fusion.16 = (f32[96,16,128]{0,2,1:T(8,128)S(1)}, f32[96,16,128]{0,2,1:T(8,128)S(1)}) fusion(f32[96,16,128]{0,2,1:T(8,128)S(1)} %copy-done.2, f32[96,18,1]{0,2,1:T(1,128)S(1)} %collective-permute-done.15, f32[96,1,128]{0,2,1:T(8,128)S(1)} %collective-permute-done.12, f32[96,1,128]{0,2,1:T(8,128)S(1)} %collective-permute-done.13, ...), kind=kLoop, calls=%fused_computation.45 | loop fusion | flops 10813440 | bytes 15078912 | tf_op jit(solution)/shard_map/add | solution.py:80
  175.7 9.6 %all-gather.1 = f32[4,2,2048]{2,1,0:T(2,128)S(1)} all-gather(f32[1,2,2048]{2,1,0:T(2,128)S(1)} %maximum_bitcast_fusion), channel_id=1, replica_groups=mesh['seg'=4,'gx'=2,'gy'=4] {'seg'}, dimensions={0}, use_global_device_ids=true | all-gather | bytes 81920 | tf_op jit(solution)/shard_map/all_gather | solution.py:138
  188.1 7.0 %pad_maximum_fusion = f32[7,96,16,128]{1,3,2,0:T(8,128)} fusion(f32[1,96,16,128]{1,3,2,0:T(8,128)S(1)} %bitcast.73, f32[6,96,16,128]{1,3,2,0:T(8,128)} %get-tuple-element.13), kind=kLoop, calls=%fused_computation.1 | loop fusion | flops 1376256 | bytes 11010048 | tf_op jit(solution)/shard_map/concatenate | solution.py:122
  195.2 7.9 %copy.49 = f32[7,96,16,128]{3,2,1,0:T(8,128)} copy(f32[7,96,16,128]{1,3,2,0:T(8,128)} %pad_maximum_fusion) | data formatting | bytes 11010048
  (139 shorter events, 36.5 us)
Async XLA Ops:
  1.5 60.1 %collective-permute-start = (f32[7,1,16,128]{3,2,1,0:T(8,128)S(1)}, f32[7,1,16,128]{3,2,1,0:T(8,128)S(1)}, u32[]{:S(2)}, u32[]{:S(2)}) collective-permute-start(f32[7,1,16,128]{3,2,1,0:T(8,128)S(1)} %get-tuple-element.19), channel_id=1, source_target_pairs={{8,0},{16,8},{24,16},{9,1},{17,9},{25,17},{10,2},{18,10},{26,18},{... | collective-permute-start | bytes 172040 | tf_op jit(solution)/shard_map/ppermute | solution.py:27
  2.8 63.3 %collective-permute-start.1 = (f32[7,1,16,128]{3,2,1,0:T(8,128)S(1)}, f32[7,1,16,128]{3,2,1,0:T(8,128)}, u32[]{:S(2)}, u32[]{:S(2)}) collective-permute-start(f32[7,1,16,128]{3,2,1,0:T(8,128)S(1)} %get-tuple-element.18), channel_id=1, source_target_pairs={{0,8},{8,16},{16,24},{1,9},{9,17},{17,25},{2,10},{10,18},{18,26},{... | collective-permute-start | bytes 172040 | tf_op jit(solution)/shard_map/ppermute | solution.py:24
  10.4 22.7 %copy-start.1 = (f32[96,16,128]{0,2,1:T(8,128)}, f32[96,16,128]{0,2,1:T(8,128)S(1)}, u32[]{:S(2)}) copy-start(f32[96,16,128]{0,2,1:T(8,128)S(1)} %copy.47) | copy-start | bytes 2359300
  11.1 139.5 %collective-permute-start.12 = (f32[96,1,128]{0,2,1:T(8,128)}, f32[96,1,128]{0,2,1:T(8,128)S(1)}, u32[]{:S(2)}, u32[]{:S(2)}) collective-permute-start(f32[96,1,128]{0,2,1:T(8,128)} %get-tuple-element.29), channel_id=1, source_target_pairs={{4,0},{5,1},{6,2},{7,3},{12,8},{13,9},{14,10},{15,11},{20,16},{21,... | collective-permute-start | bytes 147464 | tf_op jit(solution)/shard_map/ppermute | solution.py:27
  12.3 138.3 %collective-permute-start.13 = (f32[96,1,128]{0,2,1:T(8,128)S(1)}, f32[96,1,128]{0,2,1:T(8,128)S(1)}, u32[]{:S(2)}, u32[]{:S(2)}) collective-permute-start(f32[96,1,128]{0,2,1:T(8,128)S(1)} %get-tuple-element.28), channel_id=1, source_target_pairs={{0,4},{1,5},{2,6},{3,7},{8,12},{9,13},{10,14},{11,15},{16,20},{17,... | collective-permute-start | bytes 147464 | tf_op jit(solution)/shard_map/ppermute | solution.py:24
  66.1 12.3 %slice-start = ((s8[7340032]{0:T(1024)(128)(4,1)}), s8[3145728]{0:T(1024)(128)(4,1)S(1)}, s32[]{:S(2)}) async-start(s8[7340032]{0:T(1024)(128)(4,1)} %bitcast.71), calls=%async_computation | async-start | bytes 6291456
  71.2 7.1 %slice-start.1 = ((s8[7340032]{0:T(1024)(128)(4,1)}), s8[4194304]{0:T(1024)(128)(4,1)S(1)}, s32[]{:S(2)}) async-start(s8[7340032]{0:T(1024)(128)(4,1)} %bitcast.71), calls=%async_computation.1 | async-start | bytes 8388608
  71.2 8.5 %copy-start = (f32[7,1,16,128]{1,3,2,0:T(8,128)S(1)}, f32[7,1,16,128]{1,3,2,0:T(8,128)}, u32[]{:S(2)}) copy-start(f32[7,1,16,128]{1,3,2,0:T(8,128)} %copy.30) | copy-start | bytes 172036
  73.7 5.8 %collective-permute-start.2 = (f32[7,98,1,128]{1,3,2,0:T(8,128)S(1)}, f32[7,98,1,128]{1,3,2,0:T(8,128)S(1)}, u32[]{:S(2)}, u32[]{:S(2)}) collective-permute-start(f32[7,98,1,128]{1,3,2,0:T(8,128)S(1)} %get-tuple-element.17), channel_id=1, source_target_pairs={{4,0},{5,1},{6,2},{7,3},{12,8},{13,9},{14,10},{15,11},{20,16},{21,... | collective-permute-start | bytes 1053704 | tf_op jit(solution)/shard_map/ppermute | solution.py:27
  75.2 4.5 %collective-permute-start.3 = (f32[7,98,1,128]{1,3,2,0:T(8,128)S(1)}, f32[7,98,1,128]{1,3,2,0:T(8,128)S(1)}, u32[]{:S(2)}, u32[]{:S(2)}) collective-permute-start(f32[7,98,1,128]{1,3,2,0:T(8,128)S(1)} %get-tuple-element.16), channel_id=1, source_target_pairs={{0,4},{1,5},{2,6},{3,7},{8,12},{9,13},{10,14},{11,15},{16,20},{17,... | collective-permute-start | bytes 1053704 | tf_op jit(solution)/shard_map/ppermute | solution.py:24
  79.5 9.9 %copy-start.12 = (f32[6]{0:T(128)S(1)}, f32[6]{0:T(128)}, u32[]{:S(2)}) copy-start(f32[6]{0:T(128)} %constant.83.clone) | copy-start | bytes 76
  79.5 9.9 %copy-start.13 = (f32[6]{0:T(128)S(1)}, f32[6]{0:T(128)}, u32[]{:S(2)}) copy-start(f32[6]{0:T(128)} %constant.84.clone) | copy-start | bytes 76
  79.5 2.1 %copy-start.3 = (f32[7,98,1,128]{1,3,2,0:T(8,128)}, f32[7,98,1,128]{1,3,2,0:T(8,128)S(1)}, u32[]{:S(2)}) copy-start(f32[7,98,1,128]{1,3,2,0:T(8,128)S(1)} %collective-permute-done.2) | copy-start | bytes 1053700
  79.7 1.9 copy-start.5
  81.6 6.8 %collective-permute-start.4 = (f32[7,98,18,1]{1,3,2,0:T(1,128)S(1)}, f32[7,98,18,1]{1,3,2,0:T(1,128)S(1)}, u32[]{:S(2)}, u32[]{:S(2)}) collective-permute-start(f32[7,98,18,1]{1,3,2,0:T(1,128)S(1)} %get-tuple-element.15), channel_id=1, source_target_pairs={{1,0},{2,1},{3,2},{5,4},{6,5},{7,6},{9,8},{10,9},{11,10},{13,12},{... | collective-permute-start | bytes 148184 | tf_op jit(solution)/shard_map/ppermute | solution.py:27
  82.9 6.4 %collective-permute-start.5 = (f32[7,98,18,1]{1,3,2,0:T(1,128)S(1)}, f32[7,98,18,1]{1,3,2,0:T(1,128)S(1)}, u32[]{:S(2)}, u32[]{:S(2)}) collective-permute-start(f32[7,98,18,1]{1,3,2,0:T(1,128)S(1)} %get-tuple-element.14), channel_id=1, source_target_pairs={{0,1},{1,2},{2,3},{4,5},{5,6},{6,7},{8,9},{9,10},{10,11},{12,13},{... | collective-permute-start | bytes 148184 | tf_op jit(solution)/shard_map/ppermute | solution.py:24
  137.8 4.1 %copy-start.7 = (f32[96,96]{1,0:T(8,128)S(1)}, f32[96,96]{1,0:T(8,128)}, u32[]{:S(2)}) copy-start(f32[96,96]{1,0:T(8,128)} %param.12) | copy-start | bytes 110596
  138.6 4.0 %collective-permute-start.6 = (f32[1,16,128]{2,1,0:T(8,128)S(1)}, f32[1,16,128]{2,1,0:T(8,128)S(1)}, u32[]{:S(2)}, u32[]{:S(2)}) collective-permute-start(f32[1,16,128]{2,1,0:T(8,128)S(1)} %copy.37), channel_id=1, source_target_pairs={{0,8},{8,16},{16,24},{1,9},{9,17},{17,25},{2,10},{10,18},{18,26},{... | collective-permute-start | bytes 24584 | tf_op jit(solution)/shard_map/ppermute | solution.py:24
  140.6 6.7 %collective-permute-start.7 = (f32[1,16,128]{2,1,0:T(8,128)S(1)}, f32[1,16,128]{2,1,0:T(8,128)S(1)}, u32[]{:S(2)}, u32[]{:S(2)}) collective-permute-start(f32[1,16,128]{2,1,0:T(8,128)S(1)} %copy.38), channel_id=1, source_target_pairs={{8,0},{16,8},{24,16},{9,1},{17,9},{25,17},{10,2},{18,10},{26,18},{... | collective-permute-start | bytes 24584 | tf_op jit(solution)/shard_map/ppermute | solution.py:27
  147.7 15.8 %copy-start.4 = (f32[7,98,1,128]{1,3,2,0:T(8,128)S(1)}, f32[7,98,1,128]{1,3,2,0:T(8,128)}, u32[]{:S(2)}) copy-start(f32[7,98,1,128]{1,3,2,0:T(8,128)} %copy-done.3) | copy-start | bytes 1053700
  147.7 15.8 %copy-start.6 = (f32[7,98,1,128]{1,3,2,0:T(8,128)S(1)}, f32[7,98,1,128]{1,3,2,0:T(8,128)}, u32[]{:S(2)}) copy-start(f32[7,98,1,128]{1,3,2,0:T(8,128)} %copy-done.5) | copy-start | bytes 1053700
  147.9 9.9 %collective-permute-start.8 = (f32[98,1,128]{0,2,1:T(8,128)S(1)}, f32[98,1,128]{0,2,1:T(8,128)S(1)}, u32[]{:S(2)}, u32[]{:S(2)}) collective-permute-start(f32[98,1,128]{0,2,1:T(8,128)S(1)} %get-tuple-element.22), channel_id=1, source_target_pairs={{0,4},{1,5},{2,6},{3,7},{8,12},{9,13},{10,14},{11,15},{16,20},{17,... | collective-permute-start | bytes 150536 | tf_op jit(solution)/shard_map/ppermute | solution.py:24
  149.3 8.4 %collective-permute-start.9 = (f32[98,1,128]{0,2,1:T(8,128)S(1)}, f32[98,1,128]{0,2,1:T(8,128)S(1)}, u32[]{:S(2)}, u32[]{:S(2)}) collective-permute-start(f32[98,1,128]{0,2,1:T(8,128)S(1)} %get-tuple-element.23), channel_id=1, source_target_pairs={{4,0},{5,1},{6,2},{7,3},{12,8},{13,9},{14,10},{15,11},{20,16},{21,... | collective-permute-start | bytes 150536 | tf_op jit(solution)/shard_map/ppermute | solution.py:27
  151.5 16.7 %collective-permute-start.14 = (f32[96,18,1]{0,2,1:T(1,128)S(1)}, f32[96,18,1]{0,2,1:T(1,128)S(1)}, u32[]{:S(2)}, u32[]{:S(2)}) collective-permute-start(f32[96,18,1]{0,2,1:T(1,128)S(1)} %get-tuple-element.24), channel_id=1, source_target_pairs={{1,0},{2,1},{3,2},{5,4},{6,5},{7,6},{9,8},{10,9},{11,10},{13,12},{... | collective-permute-start | bytes 20744 | tf_op jit(solution)/shard_map/ppermute | solution.py:27
  152.8 15.4 %collective-permute-start.15 = (f32[96,18,1]{0,2,1:T(1,128)S(1)}, f32[96,18,1]{0,2,1:T(1,128)S(1)}, u32[]{:S(2)}, u32[]{:S(2)}) collective-permute-start(f32[96,18,1]{0,2,1:T(1,128)S(1)} %get-tuple-element.25), channel_id=1, source_target_pairs={{0,1},{1,2},{2,3},{4,5},{5,6},{6,7},{8,9},{9,10},{10,11},{12,13},{... | collective-permute-start | bytes 20744 | tf_op jit(solution)/shard_map/ppermute | solution.py:24
  157.9 8.1 %collective-permute-start.10 = (f32[98,18,1]{0,2,1:T(1,128)S(1)}, f32[98,18,1]{0,2,1:T(1,128)S(1)}, u32[]{:S(2)}, u32[]{:S(2)}) collective-permute-start(f32[98,18,1]{0,2,1:T(1,128)S(1)} %get-tuple-element.20), channel_id=1, source_target_pairs={{0,1},{1,2},{2,3},{4,5},{5,6},{6,7},{8,9},{9,10},{10,11},{12,13},{... | collective-permute-start | bytes 21176 | tf_op jit(solution)/shard_map/ppermute | solution.py:24
  161.8 6.4 %copy-start.2 = (f32[96,16,128]{0,2,1:T(8,128)S(1)}, f32[96,16,128]{0,2,1:T(8,128)}, u32[]{:S(2)}) copy-start(f32[96,16,128]{0,2,1:T(8,128)} %copy-done.1) | copy-start | bytes 2359300
  161.8 6.4 %copy-start.8 = (f32[16,128]{1,0:T(8,128)S(1)}, f32[16,128]{1,0:T(8,128)}, u32[]{:S(2)}) copy-start(f32[16,128]{1,0:T(8,128)} %param.10) | copy-start | bytes 24580
  161.8 5.7 %collective-permute-start.11 = (f32[98,18,1]{0,2,1:T(1,128)S(1)}, f32[98,18,1]{0,2,1:T(1,128)S(1)}, u32[]{:S(2)}, u32[]{:S(2)}) collective-permute-start(f32[98,18,1]{0,2,1:T(1,128)S(1)} %get-tuple-element.21), channel_id=1, source_target_pairs={{1,0},{2,1},{3,2},{5,4},{6,5},{7,6},{9,8},{10,9},{11,10},{13,12},{... | collective-permute-start | bytes 21176 | tf_op jit(solution)/shard_map/ppermute | solution.py:27
  168.2 17.2 %copy-start.11 = (f32[2,8]{1,0:T(2,128)S(1)}, f32[2,8]{1,0:T(2,128)}, u32[]{:S(2)}) copy-start(f32[2,8]{1,0:T(2,128)} %fusion.44) | copy-start | bytes 196
  168.2 18.7 %copy-start.9 = (f32[96]{0:T(128)S(1)}, f32[96]{0:T(128)}, u32[]{:S(2)}) copy-start(f32[96]{0:T(128)} %get-tuple-element.6) | copy-start | bytes 1156
  168.2 18.7 %copy-start.10 = (f32[96]{0:T(128)S(1)}, f32[96]{0:T(128)}, u32[]{:S(2)}) copy-start(f32[96]{0:T(128)} %get-tuple-element.7) | copy-start | bytes 1156
where the time goes:
time: 204 us; the launch traced here: 203 us
  other arithmetic  87.1 us (43%)
  local copies, waits for them, and re-layouts  45.7 us (22%)
  starting transfers between devices  39.8 us (20%)
  blocking collectives  19.4 us (10%)
  waiting for transfers between devices  6.94 us (3%)
  matrix products  2.19 us (1%)
    reduce_sum x1, other arithmetic, body(): mix = 0.5 * jnp.sum(species_new, axis=0)  48.4 us
    ppermute x8, starting transfers between devices, with_halo(): lax.ppermute(lax.slice_in_dim(block, block.shape[dim] - width, None, axis...  28.9 us
    unnamed x40, local copies, waits for them, and re-layouts  19.9 us
    ppermute x8, starting transfers between devices, with_halo(): lax.ppermute(lax.slice_in_dim(block, 0, width, axis=dim), axis, backward)  10.9 us
    unnamed x1, blocking collectives  9.74 us
    all_gather x1, blocking collectives, body(): lax.all_gather(ends, 'seg', axis=0, tiled=True)  9.64 us
    concatenate x1, other arithmetic, body(): gas_next = jnp.concatenate([species_new, heat_new[None]], axis=0)  7.02 us
    add x1, other arithmetic, solid_source(): temp + lateral * (beside - 4.0 * temp) + exchange[None] * (heat_new - temp)  6.22 us
  transfers between devices with their start and end apart: 16, of which 4 were waited for; matrix products, arithmetic and copies ran while one was open for 54% of the time, Pallas kernels for 0%

commit v1 on v0

--- a/solution.py
+++ b/solution.py
@@ -1,7 +1,9 @@
+import functools
 import jax
 import jax.numpy as jnp
 from jax import lax
 from jax.sharding import PartitionSpec as P
+from jax.lax import axis_index, ppermute, psum
 
 diffusion = (0.1, 0.08, 0.12, 0.09, 0.11, 0.07)
 stoich = (-1.0, -0.5, 1.0, 0.5, 0.25, 0.75)
@@ -14,6 +16,38 @@
 loss_table = (0.0, 0.3, 0.0, 0.1)
 feed_table = (0.0, 0.0, 0.4, 0.0)
 highest = lax.Precision.HIGHEST
+
+
+def get_tails(row_data, along_dim):
+    tall = psum(1, axis_name="seg")
+    a_next = axis_index("seg")
+    seen_now, reply, local_now = (tall, a_next, row_data.shape[along_dim])
+    history = []
+    for c, tick in enumerate(row_data.shape):
+        history.append(tick * seen_now if c == along_dim else tick)
+    r1 = jnp.zeros(history, row_data.dtype)
+    w_next = lax.dynamic_update_slice_in_dim(r1, row_data, reply * local_now, axis=along_dim)
+    moved = spare = row_data
+    for k in range(1, seen_now // 2 + 1):
+        inbox = []
+        for c in range(seen_now):
+            inbox.append((c, (c + 1) % seen_now))
+        moved = ppermute(moved, axis_name="seg", perm=inbox)
+        w_next = lax.dynamic_update_slice_in_dim(
+            w_next, moved, (reply - k) % seen_now * local_now, axis=along_dim
+        )
+        if 2 * k < seen_now:
+            chunks = []
+            for c in range(seen_now):
+                chunks.append((c, (c - 1) % seen_now))
+            spare = ppermute(spare, axis_name="seg", perm=chunks)
+            w_next = lax.dynamic_update_slice_in_dim(
+                w_next, spare, (reply + k) % seen_now * local_now, axis=along_dim
+            )
+    return w_next
+
+
+take_series_all_for = functools.partial(get_tails, along_dim=0)
 
 
 def with_halo(block, sides, width):
@@ -135,7 +169,7 @@
     )[None]
     segment_id = lax.axis_index("seg")
     all_ends, all_scalars = (
-        lax.all_gather(ends, "seg", axis=0, tiled=True),
+        take_series_all_for(ends),
         lax.all_gather(scalars, "seg", axis=0, tiled=True),
     )
     inverse = reduced_inverse(all_scalars)

time: 204 us -> 196 us (0.961)
  blocking collectives: 19.4 us -> 9.74 us
  starting transfers between devices: 39.8 us -> 44.9 us
  other arithmetic: 87.1 us -> 82.9 us
  waiting for transfers between devices: 6.94 us -> 9.55 us
  local copies, waits for them, and re-layouts: 45.7 us -> 43.4 us
    all_gather x1 -> x0, blocking collectives: 9.64 us -> none  [body(): lax.all_gather(ends, 'seg', axis=0, tiled=True)]
    ppermute x0 -> x3, starting transfers between devices: none -> 4.99 us  [the longest x2 4.98 us: get_tails(): moved = ppermute(moved, axis_name='seg', perm=inbox)]
    concatenate x1, other arithmetic: 7.02 us -> 3.8 us  [body(): gas_next = jnp.concatenate([species_new, heat_new[None]], axis=0)]
    ppermute x0 -> x3, waiting for transfers between devices: none -> 2.59 us  [the longest x2 2.58 us: get_tails(): moved = ppermute(moved, axis_name='seg', perm=inbox)]
    unnamed x40 -> x49, local copies, waits for them, and re-layouts: 19.9 us -> 19.2 us
  transfers between devices with their start and end apart: 16 -> 19, of which waited for: 4 -> 5; matrix products, arithmetic and copies ran while one was open for 54% -> 60% of each run, Pallas kernels for 0% -> 0%
where the time goes in v1:
time: 196 us; the launch traced here: 195 us
  other arithmetic  82.9 us (42%)
  starting transfers between devices  44.9 us (23%)
  local copies, waits for them, and re-layouts  43.4 us (22%)
  blocking collectives  9.74 us (5%)
  waiting for transfers between devices  9.55 us (5%)
  matrix products  2.2 us (1%)
    reduce_sum x1, other arithmetic, body(): mix = 0.5 * jnp.sum(species_new, axis=0)  47.5 us
    ppermute x8, starting transfers between devices, with_halo(): lax.ppermute(lax.slice_in_dim(block, block.shape[dim] - width, None, axis...  29 us
    unnamed x49, local copies, waits for them, and re-layouts  19.2 us
    ppermute x8, starting transfers between devices, with_halo(): lax.ppermute(lax.slice_in_dim(block, 0, width, axis=dim), axis, backward)  10.9 us
    unnamed x1, blocking collectives  9.74 us
    add x1, other arithmetic, solid_source(): temp + lateral * (beside - 4.0 * temp) + exchange[None] * (heat_new - temp)  6.37 us
    broadcast_in_dim x8, other arithmetic, reduced_inverse(): inverse = jnp.where(is_pivot[:, None], pivot_inv[None], inverse)  5.85 us
    ppermute x8, waiting for transfers between devices, with_halo(): lax.ppermute(lax.slice_in_dim(block, 0, width, axis=dim), axis, backward)  5.84 us
  transfers between devices with their start and end apart: 19, of which 5 were waited for; matrix products, arithmetic and copies ran while one was open for 60% of the time, Pallas kernels for 0%

profile of v1, /device:TPU:0, one launch (start us, length us, event | category | flops | bytes accessed | tf_op | source)
XLA Modules:
  0.0 194.6 jit_solution(2337731595085878039)
XLA Ops:
  2.8 6.1 %collective-permute-start.1 = (f32[7,1,16,128]{3,2,1,0:T(8,128)S(1)}, f32[7,1,16,128]{3,2,1,0:T(8,128)}, u32[]{:S(2)}, u32[]{:S(2)}) collective-permute-start(f32[7,1,16,128]{3,2,1,0:T(8,128)S(1)} %get-tuple-element.18), channel_id=1, source_target_pairs={{0,8},{8,16},{16,24},{1,9},{9,17},{17,25},{2,10},{10,18},{18,26},{... | collective-permute-start | bytes 172040 | tf_op jit(solution)/shard_map/ppermute | solution.py:58
  8.9 1.5 copy.47
  12.4 3.2 %collective-permute-start.13 = (f32[96,1,128]{0,2,1:T(8,128)S(1)}, f32[96,1,128]{0,2,1:T(8,128)S(1)}, u32[]{:S(2)}, u32[]{:S(2)}) collective-permute-start(f32[96,1,128]{0,2,1:T(8,128)S(1)} %get-tuple-element.28), channel_id=1, source_target_pairs={{0,4},{1,5},{2,6},{3,7},{8,12},{9,13},{10,14},{11,15},{16,20},{17,... | collective-permute-start | bytes 147464 | tf_op jit(solution)/shard_map/ppermute | solution.py:58
  15.6 7.9 %copy.27 = f32[7,96,16,128]{1,3,2,0:T(8,128)} copy(f32[7,96,16,128]{3,2,1,0:T(8,128)} %param.8) | data formatting | bytes 11010048 | tf_op args[0]
  26.1 3.8 %stack.12 = f32[6]{0:T(128)S(1)} concatenate(f32[1]{0:T(128)} %bitcast.7, f32[1]{0:T(128)} %bitcast.8, f32[1]{0:T(128)} %bitcast.9, f32[1]{0:T(128)} %bitcast.10, f32[1]{0:T(128)} %bitcast.11, f32[1]{0:T(128)} %bitcast.12), dimensions={0} | concatenate | bytes 48 | tf_op jit(solution)/shard_map/stack | solution.py:160
  30.2 9.7 %all-reduce = f32[24]{0:T(128)S(1)} all-reduce(f32[24]{0:T(128)S(1)} %dynamic-update-slice), channel_id=2, replica_groups=mesh['seg'=4,'gx'=2,'gy'=4] {'seg'}, use_global_device_ids=true, to_apply=%add | all-reduce | flops 24 | bytes 192
  59.3 4.5 %copy.29 = f32[7,1,16,128]{1,3,2,0:T(8,128)} copy(f32[7,1,16,128]{3,2,1,0:T(8,128)S(1)} %collective-permute-done) | data formatting | bytes 114688 | tf_op jit(solution)/shard_map/ppermute | solution.py:61
  63.8 5.2 %copy.30 = f32[7,1,16,128]{1,3,2,0:T(8,128)} copy(f32[7,1,16,128]{3,2,1,0:T(8,128)} %collective-permute-done.1) | data formatting | bytes 114688 | tf_op jit(solution)/shard_map/ppermute | solution.py:58
  69.0 2.4 %pad_maximum_fusion.33 = (f32[7,98,1,128]{1,3,2,0:T(8,128)S(1)}, f32[7,98,1,128]{1,3,2,0:T(8,128)S(1)}) fusion(f32[7,1,16,128]{1,3,2,0:T(8,128)} %copy.29, f32[7,96,16,128]{1,3,2,0:T(8,128)} %copy.27, f32[7,1,16,128]{1,3,2,0:T(8,128)} %copy.30), kind=kLoop, calls=%fused_computation.92 | loop fusion | flops 351232 | bytes 6322176 | tf_op jit(solution)/shard_map/concatenate | solution.py:62
  71.4 1.6 collective-permute-start.2
  73.0 3.1 %collective-permute-start.3 = (f32[7,98,1,128]{1,3,2,0:T(8,128)S(1)}, f32[7,98,1,128]{1,3,2,0:T(8,128)S(1)}, u32[]{:S(2)}, u32[]{:S(2)}) collective-permute-start(f32[7,98,1,128]{1,3,2,0:T(8,128)S(1)} %get-tuple-element.16), channel_id=1, source_target_pairs={{0,4},{1,5},{2,6},{3,7},{8,12},{9,13},{10,14},{11,15},{16,20},{17,... | collective-permute-start | bytes 1053704 | tf_op jit(solution)/shard_map/ppermute | solution.py:58
  77.5 1.9 pad_maximum_fusion.39
  79.4 1.3 collective-permute-start.4
  80.7 4.7 %collective-permute-start.5 = (f32[7,98,18,1]{1,3,2,0:T(1,128)S(1)}, f32[7,98,18,1]{1,3,2,0:T(1,128)S(1)}, u32[]{:S(2)}, u32[]{:S(2)}) collective-permute-start(f32[7,98,18,1]{1,3,2,0:T(1,128)S(1)} %get-tuple-element.14), channel_id=1, source_target_pairs={{0,1},{1,2},{2,3},{4,5},{5,6},{6,7},{8,9},{9,10},{10,11},{12,13},{... | collective-permute-start | bytes 148184 | tf_op jit(solution)/shard_map/ppermute | solution.py:58
  87.1 47.5 %fusion.62 = (f32[96,16,128]{0,2,1:T(8,128)S(1)}, f32[6,96,16,128]{1,3,2,0:T(8,128)}) fusion(f32[96,16,128]{0,2,1:T(8,128)} %fusion.40, f32[6]{0:T(128)} %constant.109.clone, f32[7,98,1,128]{1,3,2,0:T(8,128)} %copy-done.3, f32[7,1,16,128]{1,3,2,0:T(8,128)} %copy.29, f32[7,96,16,128]{1,3,2,0:T(8,128)} %copy.27, f32[7,1,16,128]{1,3,2,0:T(8,128)} %copy.30, ...), kind=kLoop, calls=%fused_computation.226 | loop fusion | flops 38731776 | bytes 35881976 | tf_op jit(solution)/shard_map/reduce_sum | solution.py:152
  135.4 1.7 collective-permute-start.6
  137.4 1.3 collective-permute-start.7
  139.7 4.3 %collective-permute-done.7 = f32[1,16,128]{2,1,0:T(8,128)S(1)} collective-permute-done((f32[1,16,128]{2,1,0:T(8,128)S(1)}, f32[1,16,128]{2,1,0:T(8,128)S(1)}, u32[]{:S(2)}, u32[]{:S(2)}) %collective-permute-start.7) | collective-permute-done | bytes 8224 | tf_op jit(solution)/shard_map/ppermute | solution.py:61
  144.6 1.4 collective-permute-start.8
  146.0 1.3 collective-permute-start.9
  148.2 1.3 collective-permute-start.14
  149.5 4.9 %collective-permute-start.15 = (f32[96,18,1]{0,2,1:T(1,128)S(1)}, f32[96,18,1]{0,2,1:T(1,128)S(1)}, u32[]{:S(2)}, u32[]{:S(2)}) collective-permute-start(f32[96,18,1]{0,2,1:T(1,128)S(1)} %get-tuple-element.25), channel_id=1, source_target_pairs={{0,1},{1,2},{2,3},{4,5},{5,6},{6,7},{8,9},{9,10},{10,11},{12,13},{... | collective-permute-start | bytes 20744 | tf_op jit(solution)/shard_map/ppermute | solution.py:58
  154.6 3.9 %collective-permute-start.10 = (f32[98,18,1]{0,2,1:T(1,128)S(1)}, f32[98,18,1]{0,2,1:T(1,128)S(1)}, u32[]{:S(2)}, u32[]{:S(2)}) collective-permute-start(f32[98,18,1]{0,2,1:T(1,128)S(1)} %get-tuple-element.20), channel_id=1, source_target_pairs={{0,1},{1,2},{2,3},{4,5},{5,6},{6,7},{8,9},{9,10},{10,11},{12,13},{... | collective-permute-start | bytes 21176 | tf_op jit(solution)/shard_map/ppermute | solution.py:58
  158.6 1.6 collective-permute-start.11
  160.2 2.5 %fusion.10 = f32[98,18,130]{0,2,1:T(8,128)S(1)} fusion(f32[7,98,18,1]{1,3,2,0:T(1,128)S(1)} %collective-permute-done.4, f32[7,98,18,1]{1,3,2,0:T(1,128)S(1)} %collective-permute-done.5, f32[7,98,1,128]{1,3,2,0:T(8,128)S(1)} %copy-done.4, f32[7,98,1,128]{1,3,2,0:T(8,128)S(1)} %copy-done.6, f32[7,1,16,128]{1,3,2,0:T(8,128)} %copy.29, ...), kind=kLoop, calls=%fused_computation.32 | loop fusion | flops 1375920 | bytes 7338240 | tf_op jit(solution)/shard_map/squeeze | solution.py:154
  162.8 1.5 collective-permute-done.11
  165.0 6.4 %fusion.16 = (f32[96,16,128]{0,2,1:T(8,128)S(1)}, f32[96,16,128]{0,2,1:T(8,128)S(1)}) fusion(f32[96,16,128]{0,2,1:T(8,128)S(1)} %copy-done.2, f32[96,18,1]{0,2,1:T(1,128)S(1)} %collective-permute-done.15, f32[96,1,128]{0,2,1:T(8,128)S(1)} %collective-permute-done.12, f32[96,1,128]{0,2,1:T(8,128)S(1)} %collective-permute-done.13, ...), kind=kLoop, calls=%fused_computation.45 | loop fusion | flops 10813440 | bytes 15078912 | tf_op jit(solution)/shard_map/add | solution.py:114
  172.7 3.0 %collective-permute-start.16 = (f32[2,2048]{1,0:T(2,128)S(1)}, f32[2,2048]{1,0:T(2,128)S(1)}, u32[]{:S(2)}, u32[]{:S(2)}) collective-permute-start(f32[2,2048]{1,0:T(2,128)S(1)} %get-tuple-element.38), channel_id=1, source_target_pairs={{0,8},{8,16},{16,24},{24,0},{1,9},{9,17},{17,25},{25,1},{2,10},{10... | collective-permute-start | bytes 49160 | tf_op jit(solution)/shard_map/ppermute | solution.py:35
  175.6 3.8 %pad_maximum_fusion = f32[7,96,16,128]{1,3,2,0:T(8,128)} fusion(f32[1,96,16,128]{1,3,2,0:T(8,128)S(1)} %bitcast.73, f32[6,96,16,128]{1,3,2,0:T(8,128)S(1)} %bitcast.72), kind=kLoop, calls=%fused_computation.1 | loop fusion | flops 1376256 | bytes 11010048 | tf_op jit(solution)/shard_map/concatenate | solution.py:156
  179.4 7.9 %copy.49 = f32[7,96,16,128]{3,2,1,0:T(8,128)} copy(f32[7,96,16,128]{1,3,2,0:T(8,128)} %pad_maximum_fusion) | data formatting | bytes 11010048
  187.4 2.0 %collective-permute-start.18 = (f32[2,2048]{1,0:T(2,128)S(1)}, f32[2,2048]{1,0:T(2,128)S(1)}, u32[]{:S(2)}, u32[]{:S(2)}) collective-permute-start(f32[2,2048]{1,0:T(2,128)S(1)} %collective-permute-done.16), channel_id=1, source_target_pairs={{0,8},{8,16},{16,24},{24,0},{1,9},{9,17},{17,25},{25,1},{2,10},{10... | collective-permute-start | bytes 49160 | tf_op jit(solution)/shard_map/ppermute | solution.py:35
  189.4 2.6 %collective-permute-done.18 = f32[2,2048]{1,0:T(2,128)S(1)} collective-permute-done((f32[2,2048]{1,0:T(2,128)S(1)}, f32[2,2048]{1,0:T(2,128)S(1)}, u32[]{:S(2)}, u32[]{:S(2)}) %collective-permute-start.18) | collective-permute-done | bytes 16416 | tf_op jit(solution)/shard_map/ppermute | solution.py:35
  (158 shorter events, 37.0 us)
Async XLA Ops:
  1.5 57.8 %collective-permute-start = (f32[7,1,16,128]{3,2,1,0:T(8,128)S(1)}, f32[7,1,16,128]{3,2,1,0:T(8,128)S(1)}, u32[]{:S(2)}, u32[]{:S(2)}) collective-permute-start(f32[7,1,16,128]{3,2,1,0:T(8,128)S(1)} %get-tuple-element.19), channel_id=1, source_target_pairs={{8,0},{16,8},{24,16},{9,1},{17,9},{25,17},{10,2},{18,10},{26,18},{... | collective-permute-start | bytes 172040 | tf_op jit(solution)/shard_map/ppermute | solution.py:61
  2.8 61.0 %collective-permute-start.1 = (f32[7,1,16,128]{3,2,1,0:T(8,128)S(1)}, f32[7,1,16,128]{3,2,1,0:T(8,128)}, u32[]{:S(2)}, u32[]{:S(2)}) collective-permute-start(f32[7,1,16,128]{3,2,1,0:T(8,128)S(1)} %get-tuple-element.18), channel_id=1, source_target_pairs={{0,8},{8,16},{16,24},{1,9},{9,17},{17,25},{2,10},{10,18},{18,26},{... | collective-permute-start | bytes 172040 | tf_op jit(solution)/shard_map/ppermute | solution.py:58
  10.4 13.1 %copy-start.1 = (f32[96,16,128]{0,2,1:T(8,128)}, f32[96,16,128]{0,2,1:T(8,128)S(1)}, u32[]{:S(2)}) copy-start(f32[96,16,128]{0,2,1:T(8,128)S(1)} %copy.47) | copy-start | bytes 2359300
  11.1 136.3 %collective-permute-start.12 = (f32[96,1,128]{0,2,1:T(8,128)}, f32[96,1,128]{0,2,1:T(8,128)S(1)}, u32[]{:S(2)}, u32[]{:S(2)}) collective-permute-start(f32[96,1,128]{0,2,1:T(8,128)} %get-tuple-element.29), channel_id=1, source_target_pairs={{4,0},{5,1},{6,2},{7,3},{12,8},{13,9},{14,10},{15,11},{20,16},{21,... | collective-permute-start | bytes 147464 | tf_op jit(solution)/shard_map/ppermute | solution.py:61
  12.3 11.4 %copy-start.9 = (s32[16,128]{1,0:T(8,128)S(1)}, s32[16,128]{1,0:T(8,128)}, u32[]{:S(2)}) copy-start(s32[16,128]{1,0:T(8,128)} %param.11) | copy-start | bytes 24580
  12.4 11.4 %copy-start.7 = (f32[96,96]{1,0:T(8,128)S(1)}, f32[96,96]{1,0:T(8,128)}, u32[]{:S(2)}) copy-start(f32[96,96]{1,0:T(8,128)} %param.12) | copy-start | bytes 110596
  12.4 12.0 %copy-start.12 = (f32[1,2]{1,0:T(1,128)S(1)}, f32[1,2]{1,0:T(1,128)}, u32[]{:S(2)}) copy-start(f32[1,2]{1,0:T(1,128)} %param.13) | copy-start | bytes 28
  12.4 12.6 %copy-start.15 = (u32[32]{0:T(128)S(1)}, u32[32]{0:T(128)}, u32[]{:S(2)}) copy-start(u32[32]{0:T(128)} %constant.113) | copy-start | bytes 388
  12.4 135.0 %collective-permute-start.13 = (f32[96,1,128]{0,2,1:T(8,128)S(1)}, f32[96,1,128]{0,2,1:T(8,128)S(1)}, u32[]{:S(2)}, u32[]{:S(2)}) collective-permute-start(f32[96,1,128]{0,2,1:T(8,128)S(1)} %get-tuple-element.28), channel_id=1, source_target_pairs={{0,4},{1,5},{2,6},{3,7},{8,12},{9,13},{10,14},{11,15},{16,20},{17,... | collective-permute-start | bytes 147464 | tf_op jit(solution)/shard_map/ppermute | solution.py:58
  63.8 12.3 %slice-start = ((s8[7340032]{0:T(1024)(128)(4,1)}), s8[3145728]{0:T(1024)(128)(4,1)S(1)}, s32[]{:S(2)}) async-start(s8[7340032]{0:T(1024)(128)(4,1)} %bitcast.69), calls=%async_computation | async-start | bytes 6291456
  71.4 5.8 %collective-permute-start.2 = (f32[7,98,1,128]{1,3,2,0:T(8,128)S(1)}, f32[7,98,1,128]{1,3,2,0:T(8,128)S(1)}, u32[]{:S(2)}, u32[]{:S(2)}) collective-permute-start(f32[7,98,1,128]{1,3,2,0:T(8,128)S(1)} %get-tuple-element.17), channel_id=1, source_target_pairs={{4,0},{5,1},{6,2},{7,3},{12,8},{13,9},{14,10},{15,11},{20,16},{21,... | collective-permute-start | bytes 1053704 | tf_op jit(solution)/shard_map/ppermute | solution.py:61
  73.0 4.5 %collective-permute-start.3 = (f32[7,98,1,128]{1,3,2,0:T(8,128)S(1)}, f32[7,98,1,128]{1,3,2,0:T(8,128)S(1)}, u32[]{:S(2)}, u32[]{:S(2)}) collective-permute-start(f32[7,98,1,128]{1,3,2,0:T(8,128)S(1)} %get-tuple-element.16), channel_id=1, source_target_pairs={{0,4},{1,5},{2,6},{3,7},{8,12},{9,13},{10,14},{11,15},{16,20},{17,... | collective-permute-start | bytes 1053704 | tf_op jit(solution)/shard_map/ppermute | solution.py:58
  79.4 6.9 %collective-permute-start.4 = (f32[7,98,18,1]{1,3,2,0:T(1,128)S(1)}, f32[7,98,18,1]{1,3,2,0:T(1,128)S(1)}, u32[]{:S(2)}, u32[]{:S(2)}) collective-permute-start(f32[7,98,18,1]{1,3,2,0:T(1,128)S(1)} %get-tuple-element.15), channel_id=1, source_target_pairs={{1,0},{2,1},{3,2},{5,4},{6,5},{7,6},{9,8},{10,9},{11,10},{13,12},{... | collective-permute-start | bytes 148184 | tf_op jit(solution)/shard_map/ppermute | solution.py:61
  80.7 6.4 %collective-permute-start.5 = (f32[7,98,18,1]{1,3,2,0:T(1,128)S(1)}, f32[7,98,18,1]{1,3,2,0:T(1,128)S(1)}, u32[]{:S(2)}, u32[]{:S(2)}) collective-permute-start(f32[7,98,18,1]{1,3,2,0:T(1,128)S(1)} %get-tuple-element.14), channel_id=1, source_target_pairs={{0,1},{1,2},{2,3},{4,5},{5,6},{6,7},{8,9},{9,10},{10,11},{12,13},{... | collective-permute-start | bytes 148184 | tf_op jit(solution)/shard_map/ppermute | solution.py:58
  135.4 4.0 %collective-permute-start.6 = (f32[1,16,128]{2,1,0:T(8,128)S(1)}, f32[1,16,128]{2,1,0:T(8,128)S(1)}, u32[]{:S(2)}, u32[]{:S(2)}) collective-permute-start(f32[1,16,128]{2,1,0:T(8,128)S(1)} %copy.37), channel_id=1, source_target_pairs={{0,8},{8,16},{16,24},{1,9},{9,17},{17,25},{2,10},{10,18},{18,26},{... | collective-permute-start | bytes 24584 | tf_op jit(solution)/shard_map/ppermute | solution.py:58
  137.4 6.7 %collective-permute-start.7 = (f32[1,16,128]{2,1,0:T(8,128)S(1)}, f32[1,16,128]{2,1,0:T(8,128)S(1)}, u32[]{:S(2)}, u32[]{:S(2)}) collective-permute-start(f32[1,16,128]{2,1,0:T(8,128)S(1)} %copy.38), channel_id=1, source_target_pairs={{8,0},{16,8},{24,16},{9,1},{17,9},{25,17},{10,2},{18,10},{26,18},{... | collective-permute-start | bytes 24584 | tf_op jit(solution)/shard_map/ppermute | solution.py:61
  144.4 15.8 %copy-start.4 = (f32[7,98,1,128]{1,3,2,0:T(8,128)S(1)}, f32[7,98,1,128]{1,3,2,0:T(8,128)}, u32[]{:S(2)}) copy-start(f32[7,98,1,128]{1,3,2,0:T(8,128)} %copy-done.3) | copy-start | bytes 1053700
  144.4 15.8 %copy-start.6 = (f32[7,98,1,128]{1,3,2,0:T(8,128)S(1)}, f32[7,98,1,128]{1,3,2,0:T(8,128)}, u32[]{:S(2)}) copy-start(f32[7,98,1,128]{1,3,2,0:T(8,128)} %copy-done.5) | copy-start | bytes 1053700
  144.6 9.9 %collective-permute-start.8 = (f32[98,1,128]{0,2,1:T(8,128)S(1)}, f32[98,1,128]{0,2,1:T(8,128)S(1)}, u32[]{:S(2)}, u32[]{:S(2)}) collective-permute-start(f32[98,1,128]{0,2,1:T(8,128)S(1)} %get-tuple-element.22), channel_id=1, source_target_pairs={{0,4},{1,5},{2,6},{3,7},{8,12},{9,13},{10,14},{11,15},{16,20},{17,... | collective-permute-start | bytes 150536 | tf_op jit(solution)/shard_map/ppermute | solution.py:58
  146.0 8.4 %collective-permute-start.9 = (f32[98,1,128]{0,2,1:T(8,128)S(1)}, f32[98,1,128]{0,2,1:T(8,128)S(1)}, u32[]{:S(2)}, u32[]{:S(2)}) collective-permute-start(f32[98,1,128]{0,2,1:T(8,128)S(1)} %get-tuple-element.23), channel_id=1, source_target_pairs={{4,0},{5,1},{6,2},{7,3},{12,8},{13,9},{14,10},{15,11},{20,16},{21,... | collective-permute-start | bytes 150536 | tf_op jit(solution)/shard_map/ppermute | solution.py:61
  148.2 16.7 %collective-permute-start.14 = (f32[96,18,1]{0,2,1:T(1,128)S(1)}, f32[96,18,1]{0,2,1:T(1,128)S(1)}, u32[]{:S(2)}, u32[]{:S(2)}) collective-permute-start(f32[96,18,1]{0,2,1:T(1,128)S(1)} %get-tuple-element.24), channel_id=1, source_target_pairs={{1,0},{2,1},{3,2},{5,4},{6,5},{7,6},{9,8},{10,9},{11,10},{13,12},{... | collective-permute-start | bytes 20744 | tf_op jit(solution)/shard_map/ppermute | solution.py:61
  149.5 15.4 %collective-permute-start.15 = (f32[96,18,1]{0,2,1:T(1,128)S(1)}, f32[96,18,1]{0,2,1:T(1,128)S(1)}, u32[]{:S(2)}, u32[]{:S(2)}) collective-permute-start(f32[96,18,1]{0,2,1:T(1,128)S(1)} %get-tuple-element.25), channel_id=1, source_target_pairs={{0,1},{1,2},{2,3},{4,5},{5,6},{6,7},{8,9},{9,10},{10,11},{12,13},{... | collective-permute-start | bytes 20744 | tf_op jit(solution)/shard_map/ppermute | solution.py:58
  154.6 8.1 %collective-permute-start.10 = (f32[98,18,1]{0,2,1:T(1,128)S(1)}, f32[98,18,1]{0,2,1:T(1,128)S(1)}, u32[]{:S(2)}, u32[]{:S(2)}) collective-permute-start(f32[98,18,1]{0,2,1:T(1,128)S(1)} %get-tuple-element.20), channel_id=1, source_target_pairs={{0,1},{1,2},{2,3},{4,5},{5,6},{6,7},{8,9},{9,10},{10,11},{12,13},{... | collective-permute-start | bytes 21176 | tf_op jit(solution)/shard_map/ppermute | solution.py:58
  158.6 5.7 %collective-permute-start.11 = (f32[98,18,1]{0,2,1:T(1,128)S(1)}, f32[98,18,1]{0,2,1:T(1,128)S(1)}, u32[]{:S(2)}, u32[]{:S(2)}) collective-permute-start(f32[98,18,1]{0,2,1:T(1,128)S(1)} %get-tuple-element.21), channel_id=1, source_target_pairs={{1,0},{2,1},{3,2},{5,4},{6,5},{7,6},{9,8},{10,9},{11,10},{13,12},{... | collective-permute-start | bytes 21176 | tf_op jit(solution)/shard_map/ppermute | solution.py:61
  164.9 10.7 %slice-start.2 = ((s8[6291456]{0:T(1024)(128)(4,1)}), s8[4194304]{0:T(1024)(128)(4,1)S(1)}, s32[]{:S(2)}) async-start(s8[6291456]{0:T(1024)(128)(4,1)} %bitcast.71), calls=%async_computation.2 | async-start | bytes 8388608
  165.0 10.7 %slice-start.3 = ((s8[6291456]{0:T(1024)(128)(4,1)}), s8[2097152]{0:T(1024)(128)(4,1)S(1)}, s32[]{:S(2)}) async-start(s8[6291456]{0:T(1024)(128)(4,1)} %bitcast.71), calls=%async_computation.3 | async-start | bytes 4194304
  172.7 14.7 %collective-permute-start.16 = (f32[2,2048]{1,0:T(2,128)S(1)}, f32[2,2048]{1,0:T(2,128)S(1)}, u32[]{:S(2)}, u32[]{:S(2)}) collective-permute-start(f32[2,2048]{1,0:T(2,128)S(1)} %get-tuple-element.38), channel_id=1, source_target_pairs={{0,8},{8,16},{16,24},{24,0},{1,9},{9,17},{17,25},{25,1},{2,10},{10... | collective-permute-start | bytes 49160 | tf_op jit(solution)/shard_map/ppermute | solution.py:35
  175.6 13.8 %collective-permute-start.17 = (f32[2,2048]{1,0:T(2,128)S(1)}, f32[2,2048]{1,0:T(2,128)S(1)}, u32[]{:S(2)}, u32[]{:S(2)}) collective-permute-start(f32[2,2048]{1,0:T(2,128)S(1)} %get-tuple-element.38), channel_id=1, source_target_pairs={{0,24},{8,0},{16,8},{24,16},{1,25},{9,1},{17,9},{25,17},{2,26},{10... | collective-permute-start | bytes 49160 | tf_op jit(solution)/shard_map/ppermute | solution.py:43
  179.4 12.6 %copy-start.13 = (f32[2,8]{1,0:T(2,128)S(1)}, f32[2,8]{1,0:T(2,128)}, u32[]{:S(2)}) copy-start(f32[2,8]{1,0:T(2,128)} %fusion.44) | copy-start | bytes 196
  179.4 13.9 %copy-start.10 = (f32[96]{0:T(128)S(1)}, f32[96]{0:T(128)}, u32[]{:S(2)}) copy-start(f32[96]{0:T(128)} %get-tuple-element.6) | copy-start | bytes 1156
  179.4 14.0 %copy-start.11 = (f32[96]{0:T(128)S(1)}, f32[96]{0:T(128)}, u32[]{:S(2)}) copy-start(f32[96]{0:T(128)} %get-tuple-element.7) | copy-start | bytes 1156
  187.4 4.6 %collective-permute-start.18 = (f32[2,2048]{1,0:T(2,128)S(1)}, f32[2,2048]{1,0:T(2,128)S(1)}, u32[]{:S(2)}, u32[]{:S(2)}) collective-permute-start(f32[2,2048]{1,0:T(2,128)S(1)} %collective-permute-done.16), channel_id=1, source_target_pairs={{0,8},{8,16},{16,24},{24,0},{1,9},{9,17},{17,25},{25,1},{2,10},{10... | collective-permute-start | bytes 49160 | tf_op jit(solution)/shard_map/ppermute | solution.py:35
  (8 other events, 50.5 us)
